TPU v7x, 256 devices: a whole 4x4x8 slice. The times are simulated.
256 devices in a mesh: row: 8 (over y, core), col: 8 (over z), track: 4 (over x).
Axes of the slice: x: 4, y: 4, z: 8, core: 2. Of those that a mesh axis runs over, the one named last changes fastest.
Arguments:
- factors: float32 [16384, 2, 16, 576], P(('row', 'col', 'track')), may hold values from -0.5 to 0.5
- track_clusters: int32 [16384, 2], P(('row', 'col', 'track')), may hold values from 0 to 7, as said below
- filed_flip: int32 [16384], P(('row', 'col', 'track')), may hold values from 0 to 1, as said below
- damping: float32 [8, 576], P('row'), may hold values from 50 to 500
- rhs: float32 [8, 576], P('row'), may hold values from -3000 to 3000
Outputs:
- solution: float32 [8, 576], P('row')
- scaled_residual: float32 [8, 576], P('row')
- filed_blocks: float32 [8, 8, 576, 576], P('row', 'col', 'track')
Inputs may be any that keep to these rules, and one draw needn't show every extreme that they name: `track_clusters`: each row names two different clusters, the first below the second. `filed_flip`: the owner of a block filed under (i, j) is the device of row group i // 1 and column j, with the track index of the device that holds the track block. Of the 64 track blocks of one device at most 3 go to any one owner, and in every draw, for each track index, some owner receives exactly 3 from every device of that track index.
All inputs are finite; a program needn't handle non-finite values.
Results may differ from a plain program's by a relative error of at most 0.0003.
Values sent between devices are 32-bit elements; how exact they have to be, the bound alone decides.
No kernel may reach another device: no remote copies, remote signals or barrier semaphores. Data moves between devices by JAX's collectives and lax.ppermute only.
A program may use at most 128 MiB of HBM per device.

v0:
```python
import jax
import jax.numpy as jnp
from jax import lax
from jax.sharding import PartitionSpec as P

ITERS = 2
highest = lax.Precision.HIGHEST


def fitness_sum(residual, scaled):
    return lax.psum(jnp.sum(residual * scaled), "row")


def on_device(factors, track_clusters, filed_flip, damping, rhs):
    n_row = lax.axis_size("row")
    n_col = lax.axis_size("col")
    n_track = lax.axis_size("track")
    owners = n_row * n_col
    tb_dev = factors.shape[0]
    jac_rows = factors.shape[2]
    params = factors.shape[3]
    row_clusters = damping.shape[0]
    clusters = row_clusters * n_row
    capacity = 3 * tb_dev // owners
    row_share = params // n_track
    row_id = lax.axis_index("row")
    col_id = lax.axis_index("col")
    track_id = lax.axis_index("track")
    low_cluster = track_clusters[:, 0]
    high_cluster = track_clusters[:, 1]
    low_side = factors[:, 0]
    high_side = factors[:, 1]
    cluster_ids = jnp.arange(clusters, dtype=jnp.int32)
    low_onehot = (low_cluster[:, None] == cluster_ids[None, :]).astype(jnp.float32)
    high_onehot = (high_cluster[:, None] == cluster_ids[None, :]).astype(jnp.float32)
    diag_part = jnp.dot(low_onehot.T, jnp.sum(low_side * low_side, axis=1), precision=highest)
    diag_part = diag_part + jnp.dot(
        high_onehot.T, jnp.sum(high_side * high_side, axis=1), precision=highest
    )
    diag_all = lax.psum(diag_part, ("row", "col", "track"))
    precond = damping + lax.dynamic_slice_in_dim(diag_all, row_id * row_clusters, row_clusters, 0)
    flipped = filed_flip == 1
    filed_row = jnp.where(flipped, high_cluster, low_cluster)
    filed_col = jnp.where(flipped, low_cluster, high_cluster)
    oriented = jnp.where(flipped[:, None, None, None], factors[:, ::-1], factors)
    owner_row = filed_row // row_clusters
    target = owner_row * n_col + filed_col
    slot_ids = filed_row - owner_row * row_clusters
    owner_hits = (target[:, None] == jnp.arange(owners, dtype=jnp.int32)[None, :]).astype(jnp.int32)
    places = jnp.sum((jnp.cumsum(owner_hits, axis=0) - 1) * owner_hits, axis=1)
    position = target * capacity + places
    outgoing = (
        jnp.zeros((owners * capacity, 2, jac_rows, params), jnp.float32).at[position].set(oriented)
    )
    outgoing_slots = jnp.zeros((owners * capacity,), jnp.int32).at[position].set(slot_ids)
    incoming, incoming_slots = (
        lax.all_to_all(
            outgoing.reshape(owners, capacity, 2, jac_rows, params),
            ("row", "col"),
            split_axis=0,
            concat_axis=0,
            tiled=True,
        ),
        lax.all_to_all(
            outgoing_slots.reshape(owners, capacity),
            ("row", "col"),
            split_axis=0,
            concat_axis=0,
            tiled=True,
        ),
    )
    received = incoming.reshape(owners * capacity, 2, jac_rows, params)
    received_slots = incoming_slots.reshape(owners * capacity)
    received_rows = received[:, 0]
    received_cols = received[:, 1]
    slot_masks = [(received_slots == 0).astype(jnp.float32)]
    pieces = [
        jnp.einsum(
            "mkr,mkc->rc",
            received_rows * slot_mask[:, None, None],
            received_cols,
            precision=highest,
            preferred_element_type=jnp.float32,
        )
        for slot_mask in slot_masks
    ]
    filed = lax.psum_scatter(pieces[0], "track", scatter_dimension=0, tiled=True)
    filed_blocks = filed.reshape(row_share, row_clusters, params)
    blocks_out = jnp.transpose(filed_blocks, (1, 0, 2))[:, None]
    col_onehot = (cluster_ids == col_id).astype(jnp.float32)
    solution = jnp.zeros_like(rhs)
    residual = rhs
    scaled = residual / precond
    direction = scaled
    fitness = fitness_sum(residual, scaled)
    for iteration in range(ITERS):
        full_dir = lax.all_gather(direction, "row", axis=0, tiled=True)
        col_dir = jnp.dot(col_onehot, full_dir, precision=highest)
        own_share = lax.dynamic_slice_in_dim(direction, track_id * row_share, row_share, 1)
        row_terms = jnp.einsum("rsc,c->sr", filed_blocks, col_dir, precision=highest)
        col_terms = jnp.einsum("rsc,sr->c", filed_blocks, own_share, precision=highest)
        low_dir = jnp.dot(low_onehot, full_dir, precision=highest)
        high_dir = jnp.dot(high_onehot, full_dir, precision=highest)
        low_proj = jnp.einsum("mkc,mc->mk", low_side, low_dir, precision=highest)
        high_proj = jnp.einsum("mkc,mc->mk", high_side, high_dir, precision=highest)
        low_back = jnp.einsum("mk,mkc->mc", low_proj, low_side, precision=highest)
        high_back = jnp.einsum("mk,mkc->mc", high_proj, high_side, precision=highest)
        local = jnp.dot(low_onehot.T, low_back, precision=highest) + jnp.dot(
            high_onehot.T, high_back, precision=highest
        )
        placed = lax.dynamic_update_slice(
            jnp.zeros((clusters, params), jnp.float32),
            row_terms,
            (row_id * row_clusters, track_id * row_share),
        )
        local = local + placed + col_onehot[:, None] * col_terms[None, :]
        summed = lax.psum(local, ("row", "col", "track"))
        images = (
            lax.dynamic_slice_in_dim(summed, row_id * row_clusters, row_clusters, 0)
            + damping * direction
        )
        curvature = lax.psum(jnp.sum(direction * images), "row")
        images, curvature = (images, curvature)
        step_size = fitness / curvature
        solution = solution + step_size * direction
        residual = residual - step_size * images
        scaled = residual / precond
        fitness_next = fitness_sum(residual, scaled)
        direction = scaled + fitness_next / fitness * direction
        fitness = fitness_next
    return (solution, scaled, blocks_out)


def solution(mesh):
    in_specs = (
        P(("row", "col", "track"), None, None, None),
        P(("row", "col", "track"), None),
        P(("row", "col", "track")),
        P("row", None),
        P("row", None),
    )
    out_specs = (P("row", None), P("row", None), P("row", "col", "track", None))
    return jax.shard_map(
        on_device, mesh=mesh, in_specs=in_specs, out_specs=out_specs, check_vma=False
    )
```

profile of v0, /device:TPU:1, one launch (start us, length us, event | category | flops | bytes accessed | tf_op | source)
XLA Modules:
  0.0 1023.1 jit_solution(7229425490721513363)
XLA Ops:
  7.2 0.8 select_add_fusion
  7.9 0.1 fusion.59
  8.0 0.1 reduce_window_sum.11
  8.1 0.2 select_reduce_fusion
  8.3 0.8 scatter_custom_fusion.1
  9.1 0.8 all_to_all.10
  9.8 13.1 %all-to-all-start.1 = ((s32[64,1,3]{2,1,0:T(1,128)}), s32[64,1,3]{2,1,0:T(1,128)S(1)}, u32[]{:S(2)}, u32[]{:S(2)}) async-start(s32[64,1,3]{2,1,0:T(1,128)} %bitcast.21), calls=%async_computation.1 | async-start | bytes 65536 | tf_op jit(solution)/shard_map/all_to_all | solution.py:64
  23.0 0.7 broadcast_compare_fusion
  23.7 6.9 reverse_select_fusion
  30.5 7.5 broadcast_in_dim.12
  38.0 13.0 %scatter_fusion = f32[192,2,16,576]{3,2,1,0:T(8,128)} fusion(f32[192,2,16,576]{3,2,1,0:T(8,128)} %broadcast_in_dim.12, s32[64]{0:T(128)S(1)} %compare_select_fusion, f32[64,2,16,576]{3,2,1,0:T(8,128)} %reverse_select_fusion), kind=kCustom, calls=%fused_computation | custom fusion | bytes 14156032 | tf_op jit(solution)/shard_map/scatter | solution.py:53
  51.1 10.7 %all-to-all-start = ((f32[64,3,2,16,576]{4,3,2,1,0:T(8,128)}), f32[64,3,2,16,576]{4,3,2,1,0:T(8,128)}, u32[]{:S(2)}, u32[]{:S(2)}) async-start(f32[64,3,2,16,576]{4,3,2,1,0:T(8,128)} %bitcast.149), calls=%async_computation | async-start | bytes 31457280 | tf_op jit(solution)/shard_map/all_to_all | solution.py:57
  61.8 0.0 reduce-scatter.2.cloned.1.call-start
  61.9 3.6 fusion.11
  65.4 0.3 fusion.60
  65.7 0.1 fusion.58
  65.8 0.1 reshape.60
  66.0 344.5 %all-to-all-done = f32[64,3,2,16,576]{4,3,2,1,0:T(8,128)} async-done(((f32[64,3,2,16,576]{4,3,2,1,0:T(8,128)}), f32[64,3,2,16,576]{4,3,2,1,0:T(8,128)}, u32[]{:S(2)}, u32[]{:S(2)}) %all-to-all-start) | async-done | bytes 14155808 | tf_op jit(solution)/shard_map/all_to_all | solution.py:57
  410.5 3.8 slice.25
  414.2 3.8 fusion
  418.1 0.0 copy-start.1
  418.1 0.0 copy-start.2
  418.1 247.6 %fusion.29 = f32[576,576]{1,0:T(8,128)} fusion(f32[192,1,16,576]{3,2,1,0:T(8,128)S(1)} %slice.25, f32[192,16,576]{2,1,0:T(8,128)S(1)} %fusion), kind=kOutput, calls=%fused_computation.36 | convolution fusion | flops 12230590464 | bytes 15482880 | tf_op jit(solution)/shard_map/mkr,mkc->rc/dot_general | solution.py:78
  665.7 0.0 reduce-scatter.2.cloned.1.call-update
  665.7 0.3 convolution_add_fusion.2
  666.0 89.9 %psum.49 = f32[8,576]{1,0:T(8,128)S(1)} all-reduce(f32[8,576]{1,0:T(8,128)S(1)} %convolution_add_fusion.2), channel_id=1, replica_groups=mesh['row'=8,'col'=8,'track'=4] {'row','col','track'}, use_global_device_ids=true, to_apply=%region_2.0 | all-reduce | flops 4608 | bytes 36864 | tf_op jit(solution)/shard_map/psum | solution.py:40
  755.9 13.4 %all-gather = f32[8,1,576]{2,1,0:T(1,128)S(1)} all-gather(f32[1,1,576]{2,1,0:T(1,128)S(1)} %bitcast.151), channel_id=1, replica_groups=mesh['row'=8,'col'=8,'track'=4] {'row'}, dimensions={0}, use_global_device_ids=true | all-gather | bytes 20736 | tf_op jit(solution)/shard_map/all_gather | solution.py:97
  769.4 0.3 convolution_bitcast_fusion.3
  769.6 0.3 convolution_bitcast_fusion.2
  769.9 0.1 convolution_bitcast_fusion.5
  770.0 5.1 fusion.32
  775.2 3.3 fusion.16
  778.5 0.3 fusion.48
  778.7 5.1 fusion.38
  783.9 3.4 fusion.7
  787.2 0.3 convolution_add_fusion.1
  787.5 0.0 reduce-scatter.2.cloned.1.call-done
  787.6 1.4 convolution_add_fusion.4
  789.0 0.2 add.92
  789.2 1.3 convolution_reduce_fusion.1
  790.6 0.1 multiply_add_fusion.1
  790.7 73.0 %psum.51 = f32[8,576]{1,0:T(8,128)S(1)} all-reduce(f32[8,576]{1,0:T(8,128)S(1)} %multiply_add_fusion.1), channel_id=1, replica_groups=mesh['row'=8,'col'=8,'track'=4] {'row','col','track'}, use_global_device_ids=true, to_apply=%region_10.11 | all-reduce | flops 4608 | bytes 36864 | tf_op jit(solution)/shard_map/psum | solution.py:117
  863.6 0.6 multiply_reduce_fusion.2
  864.3 13.1 %all-reduce = (f32[]{:T(128)}, f32[]{:T(128)}) all-reduce(f32[]{:T(128)} %get-tuple-element.6, f32[]{:T(128)} %get-tuple-element.5), channel_id=1, replica_groups=mesh['row'=8,'col'=8,'track'=4] {'row'}, use_global_device_ids=true, to_apply=%region_4.5 | all-reduce | flops 2 | bytes 16 | tf_op jit(solution)/shard_map/psum | solution.py:11
  878.7 0.6 multiply_reduce_fusion.1
  879.3 15.3 %psum.53 = f32[]{:T(128)} all-reduce(f32[]{:T(128)} %get-tuple-element.9), channel_id=1, replica_groups=mesh['row'=8,'col'=8,'track'=4] {'row'}, use_global_device_ids=true, to_apply=%region_14.15 | all-reduce | flops 1 | bytes 8 | tf_op jit(solution)/shard_map/psum | solution.py:11
  895.9 13.4 %all-gather.1 = f32[8,1,576]{2,1,0:T(1,128)S(1)} all-gather(f32[1,1,576]{2,1,0:T(1,128)S(1)} %bitcast.152), channel_id=1, replica_groups=mesh['row'=8,'col'=8,'track'=4] {'row'}, dimensions={0}, use_global_device_ids=true | all-gather | bytes 20736 | tf_op jit(solution)/shard_map/all_gather | solution.py:97
  909.3 0.3 convolution_bitcast_fusion.1
  909.6 0.3 convolution_bitcast_fusion
  909.9 0.1 convolution_bitcast_fusion.4
  910.0 5.3 fusion.35
  915.3 3.3 fusion.12
  918.6 0.3 fusion.45
  918.9 5.1 fusion.41
  924.0 1.5 fusion.3
  925.6 0.3 convolution_add_fusion
  925.9 0.4 convolution_add_fusion.3
  926.3 0.2 add.98
  926.5 0.4 convolution_reduce_fusion
  926.9 0.1 multiply_add_fusion
  927.0 73.7 %psum.54 = f32[8,576]{1,0:T(8,128)S(1)} all-reduce(f32[8,576]{1,0:T(8,128)S(1)} %multiply_add_fusion), channel_id=1, replica_groups=mesh['row'=8,'col'=8,'track'=4] {'row','col','track'}, use_global_device_ids=true, to_apply=%region_15.16 | all-reduce | flops 4608 | bytes 36864 | tf_op jit(solution)/shard_map/psum | solution.py:117
  1000.7 0.6 multiply_reduce_fusion
  1001.3 13.1 %psum.55 = f32[]{:T(128)} all-reduce(f32[]{:T(128)} %multiply_reduce_fusion), channel_id=1, replica_groups=mesh['row'=8,'col'=8,'track'=4] {'row'}, use_global_device_ids=true, to_apply=%region_17.18 | all-reduce | flops 1 | bytes 8 | tf_op jit(solution)/shard_map/psum | solution.py:122
  1015.7 0.6 subtract_divide_fusion
  (18 shorter events, 0.1 us)
Async XLA Ops:
  9.8 41.2 %all-to-all-start.1 = ((s32[64,1,3]{2,1,0:T(1,128)}), s32[64,1,3]{2,1,0:T(1,128)S(1)}, u32[]{:S(2)}, u32[]{:S(2)}) async-start(s32[64,1,3]{2,1,0:T(1,128)} %bitcast.21), calls=%async_computation.1 | async-start | bytes 65536 | tf_op jit(solution)/shard_map/all_to_all | solution.py:64
  51.0 10.8 %copy-start.3 = (s32[64,2]{0,1:T(2,128)S(1)}, s32[64,2]{0,1:T(2,128)}, u32[]{:S(2)}) copy-start(s32[64,2]{0,1:T(2,128)} %param.6) | copy-start | bytes 1540
  51.1 359.4 %all-to-all-start = ((f32[64,3,2,16,576]{4,3,2,1,0:T(8,128)}), f32[64,3,2,16,576]{4,3,2,1,0:T(8,128)}, u32[]{:S(2)}, u32[]{:S(2)}) async-start(f32[64,3,2,16,576]{4,3,2,1,0:T(8,128)} %bitcast.149), calls=%async_computation | async-start | bytes 31457280 | tf_op jit(solution)/shard_map/all_to_all | solution.py:57
  61.8 725.8 %reduce-scatter.2.cloned.1.call-start = ((), (), s32[]{:S(2)}) async-start(), calls=%async_computation.3 | async-start | bytes 1843200 | tf_op jit(solution)/shard_map/reduce_scatter | solution.py:87
  418.1 337.9 %copy-start.1 = (f32[1,576]{1,0:T(1,128)S(1)}, f32[1,576]{1,0:T(1,128)}, u32[]{:S(2)}) copy-start(f32[1,576]{1,0:T(1,128)} %param.8) | copy-start | bytes 6916
  418.1 337.8 %copy-start.2 = (f32[1,576]{1,0:T(1,128)S(1)}, f32[1,576]{1,0:T(1,128)}, u32[]{:S(2)}) copy-start(f32[1,576]{1,0:T(1,128)} %param.9) | copy-start | bytes 6916
  783.9 140.1 %slice-start = ((s8[5242880]{0:T(1024)(128)(4,1)}), s8[1048576]{0:T(1024)(128)(4,1)S(1)}, s32[]{:S(2)}) async-start(s8[5242880]{0:T(1024)(128)(4,1)} %bitcast.147), calls=%async_computation.4 | async-start | bytes 2097152
  910.0 14.0 %slice-start.1 = ((s8[5242880]{0:T(1024)(128)(4,1)}), s8[4194304]{0:T(1024)(128)(4,1)S(1)}, s32[]{:S(2)}) async-start(s8[5242880]{0:T(1024)(128)(4,1)} %bitcast.147), calls=%async_computation.5 | async-start | bytes 8388608
  910.0 15.8 %copy-start = (f32[144,576]{1,0:T(8,128)S(1)}, f32[144,576]{1,0:T(8,128)}, u32[]{:S(2)}) copy-start(f32[144,576]{1,0:T(8,128)} %reduce-scatter.2.cloned.1.call-done) | copy-start | bytes 995332
Sparse Core Ops, SparseCore 0:
  665.8 38.9 reduce-scatter.1
where the time goes:
time: 1020 us
  waiting for transfers between devices  345 us (34%)
  blocking collectives  305 us (30%)
  matrix products  286 us (28%)
  local copies, waits for them, and re-layouts  26.5 us (3%)
  starting transfers between devices  23.9 us (2%)
  other arithmetic  18.8 us (2%)
  between operations  18.3 us (2%)
    all_to_all x1, waiting for transfers between devices, on_device(): lax.all_to_all(outgoing.reshape(owners, capacity, 2, jac_rows, params), (...  345 us
    dot_general x1, matrix products, on_device(): jnp.einsum('mkr,mkc->rc', received_rows * slot_mask[:, None, None], recei...  248 us
    psum x2, blocking collectives, on_device(): summed = lax.psum(local, ('row', 'col', 'track'))  147 us
    psum x1, blocking collectives, on_device(): diag_all = lax.psum(diag_part, ('row', 'col', 'track'))  89.9 us
    psum x2, blocking collectives, fitness_sum(): return lax.psum(jnp.sum(residual * scaled), 'row')  28.3 us
    all_gather x2, blocking collectives, on_device(): full_dir = lax.all_gather(direction, 'row', axis=0, tiled=True)  26.8 us
  transfers between devices with their start and end apart: 3, of which 1 were waited for; matrix products, arithmetic and copies ran while one was open for 5% of the time, Pallas kernels for 0%

commit v1 on v0

--- a/solution.py
+++ b/solution.py
@@ -114,7 +114,7 @@
             (row_id * row_clusters, track_id * row_share),
         )
         local = local + placed + col_onehot[:, None] * col_terms[None, :]
-        summed = lax.psum(local, ("row", "col", "track"))
+        summed = lax.psum(lax.psum(local, "row"), ("col", "track"))
         images = (
             lax.dynamic_slice_in_dim(summed, row_id * row_clusters, row_clusters, 0)
             + damping * direction

time: 1020 us -> 1200 us (1.18)
  blocking collectives: 305 us -> 479 us
    psum x2 -> x4, blocking collectives: 147 us -> 263 us  [on_device(): summed = lax.psum(lax.psum(local, 'row'), ('col', 'track'))]
    psum x1, blocking collectives: 13.1 us -> 43.2 us  [on_device(): curvature = lax.psum(jnp.sum(direction * images), 'row')]
    psum x2, blocking collectives: 28.3 us -> 56.3 us  [fitness_sum(): return lax.psum(jnp.sum(residual * scaled), 'row')]
  transfers between devices with their start and end apart: 3 -> 3, of which waited for: 1 -> 1; matrix products, arithmetic and copies ran while one was open for 5% -> 4% of each run, Pallas kernels for 0% -> 0%
where the time goes in v1:
time: 1200 us
  blocking collectives  479 us (40%)
  waiting for transfers between devices  345 us (29%)
  matrix products  286 us (24%)
  local copies, waits for them, and re-layouts  26.5 us (2%)
  starting transfers between devices  23.9 us (2%)
  other arithmetic  18.8 us (2%)
  between operations  18.3 us (2%)
    all_to_all x1, waiting for transfers between devices, on_device(): lax.all_to_all(outgoing.reshape(owners, capacity, 2, jac_rows, params), (...  345 us
    psum x4, blocking collectives, on_device(): summed = lax.psum(lax.psum(local, 'row'), ('col', 'track'))  263 us
    dot_general x1, matrix products, on_device(): jnp.einsum('mkr,mkc->rc', received_rows * slot_mask[:, None, None], recei...  248 us
    psum x1, blocking collectives, on_device(): diag_all = lax.psum(diag_part, ('row', 'col', 'track'))  89.9 us
    psum x2, blocking collectives, fitness_sum(): return lax.psum(jnp.sum(residual * scaled), 'row')  56.3 us
    psum x1, blocking collectives, on_device(): curvature = lax.psum(jnp.sum(direction * images), 'row')  43.2 us
    all_gather x2, blocking collectives, on_device(): full_dir = lax.all_gather(direction, 'row', axis=0, tiled=True)  26.8 us
  transfers between devices with their start and end apart: 3, of which 1 were waited for; matrix products, arithmetic and copies ran while one was open for 4% of the time, Pallas kernels for 0%

profile of v1, /device:TPU:1, one launch (start us, length us, event | category | flops | bytes accessed | tf_op | source)
XLA Modules:
  0.0 1197.7 jit_solution(5563441984257847334)
XLA Ops:
  7.2 0.8 select_add_fusion
  7.9 0.1 fusion.59
  8.0 0.1 reduce_window_sum.11
  8.1 0.2 select_reduce_fusion
  8.3 0.8 scatter_custom_fusion.1
  9.1 0.8 all_to_all.10
  9.8 13.1 %all-to-all-start.1 = ((s32[64,1,3]{2,1,0:T(1,128)}), s32[64,1,3]{2,1,0:T(1,128)S(1)}, u32[]{:S(2)}, u32[]{:S(2)}) async-start(s32[64,1,3]{2,1,0:T(1,128)} %bitcast.21), calls=%async_computation.1 | async-start | bytes 65536 | tf_op jit(solution)/shard_map/all_to_all | solution.py:64
  23.0 0.7 broadcast_compare_fusion
  23.7 6.9 reverse_select_fusion
  30.5 7.5 broadcast_in_dim.12
  38.0 13.0 %scatter_fusion = f32[192,2,16,576]{3,2,1,0:T(8,128)} fusion(f32[192,2,16,576]{3,2,1,0:T(8,128)} %broadcast_in_dim.12, s32[64]{0:T(128)S(1)} %compare_select_fusion, f32[64,2,16,576]{3,2,1,0:T(8,128)} %reverse_select_fusion), kind=kCustom, calls=%fused_computation | custom fusion | bytes 14156032 | tf_op jit(solution)/shard_map/scatter | solution.py:53
  51.1 10.7 all-to-all-start
  61.8 0.0 reduce-scatter.2.cloned.1.call-start
  61.9 3.6 fusion.11
  65.4 0.3 fusion.60
  65.7 0.1 fusion.58
  65.8 0.1 reshape.60
  66.0 344.5 %all-to-all-done = f32[64,3,2,16,576]{4,3,2,1,0:T(8,128)} async-done(((f32[64,3,2,16,576]{4,3,2,1,0:T(8,128)}), f32[64,3,2,16,576]{4,3,2,1,0:T(8,128)}, u32[]{:S(2)}, u32[]{:S(2)}) %all-to-all-start) | async-done | bytes 14155808 | tf_op jit(solution)/shard_map/all_to_all | solution.py:57
  410.5 3.8 slice.25
  414.2 3.8 fusion
  418.1 247.6 %fusion.29 = f32[576,576]{1,0:T(8,128)} fusion(f32[192,1,16,576]{3,2,1,0:T(8,128)S(1)} %slice.25, f32[192,16,576]{2,1,0:T(8,128)S(1)} %fusion), kind=kOutput, calls=%fused_computation.36 | convolution fusion | flops 12230590464 | bytes 15482880 | tf_op jit(solution)/shard_map/mkr,mkc->rc/dot_general | solution.py:78
  665.7 0.0 reduce-scatter.2.cloned.1.call-update
  665.7 0.3 convolution_add_fusion.2
  666.0 89.9 %psum.63 = f32[8,576]{1,0:T(8,128)S(1)} all-reduce(f32[8,576]{1,0:T(8,128)S(1)} %convolution_add_fusion.2), channel_id=1, replica_groups=mesh['row'=8,'col'=8,'track'=4] {'row','col','track'}, use_global_device_ids=true, to_apply=%region_2.0 | all-reduce | flops 4608 | bytes 36864 | tf_op jit(solution)/shard_map/psum | solution.py:40
  755.9 13.4 %all-gather = f32[8,1,576]{2,1,0:T(1,128)S(1)} all-gather(f32[1,1,576]{2,1,0:T(1,128)S(1)} %bitcast.151), channel_id=1, replica_groups=mesh['row'=8,'col'=8,'track'=4] {'row'}, dimensions={0}, use_global_device_ids=true | all-gather | bytes 20736 | tf_op jit(solution)/shard_map/all_gather | solution.py:97
  769.4 0.3 convolution_bitcast_fusion.3
  769.6 0.3 convolution_bitcast_fusion.2
  769.9 0.1 convolution_bitcast_fusion.5
  770.0 5.1 fusion.32
  775.2 3.3 fusion.16
  778.5 0.3 fusion.48
  778.7 5.1 fusion.38
  783.9 3.4 fusion.7
  787.2 0.3 convolution_add_fusion.1
  787.5 0.0 reduce-scatter.2.cloned.1.call-done
  787.6 1.4 convolution_add_fusion.4
  789.0 0.2 add.96
  789.2 1.3 convolution_reduce_fusion.1
  790.6 0.1 multiply_add_fusion.1
  790.7 22.1 %psum.65 = f32[8,576]{1,0:T(8,128)S(1)} all-reduce(f32[8,576]{1,0:T(8,128)S(1)} %multiply_add_fusion.1), channel_id=1, replica_groups=mesh['row'=8,'col'=8,'track'=4] {'row'}, use_global_device_ids=true, to_apply=%region_10.11 | all-reduce | flops 4608 | bytes 36864 | tf_op jit(solution)/shard_map/psum | solution.py:117
  812.7 110.4 %psum.66 = f32[8,576]{1,0:T(8,128)S(1)} all-reduce(f32[8,576]{1,0:T(8,128)S(1)} %psum.65), channel_id=1, replica_groups=mesh['row'=8,'col'=8,'track'=4] {'col','track'}, use_global_device_ids=true, to_apply=%region_11.12 | all-reduce | flops 4608 | bytes 36864 | tf_op jit(solution)/shard_map/psum | solution.py:117
  923.1 0.6 multiply_reduce_fusion.2
  923.7 43.3 %all-reduce = (f32[]{:T(128)}, f32[]{:T(128)}) all-reduce(f32[]{:T(128)} %get-tuple-element.6, f32[]{:T(128)} %get-tuple-element.5), channel_id=1, replica_groups=mesh['row'=8,'col'=8,'track'=4] {'row'}, use_global_device_ids=true, to_apply=%region_4.5 | all-reduce | flops 2 | bytes 16 | tf_op jit(solution)/shard_map/psum | solution.py:11
  968.3 0.6 multiply_reduce_fusion.1
  968.9 13.0 %psum.68 = f32[]{:T(128)} all-reduce(f32[]{:T(128)} %get-tuple-element.9), channel_id=1, replica_groups=mesh['row'=8,'col'=8,'track'=4] {'row'}, use_global_device_ids=true, to_apply=%region_15.16 | all-reduce | flops 1 | bytes 8 | tf_op jit(solution)/shard_map/psum | solution.py:11
  983.3 13.4 %all-gather.1 = f32[8,1,576]{2,1,0:T(1,128)S(1)} all-gather(f32[1,1,576]{2,1,0:T(1,128)S(1)} %bitcast.152), channel_id=1, replica_groups=mesh['row'=8,'col'=8,'track'=4] {'row'}, dimensions={0}, use_global_device_ids=true | all-gather | bytes 20736 | tf_op jit(solution)/shard_map/all_gather | solution.py:97
  996.7 0.3 convolution_bitcast_fusion.1
  997.0 0.3 convolution_bitcast_fusion
  997.3 0.1 convolution_bitcast_fusion.4
  997.4 5.3 fusion.35
  1002.7 3.3 fusion.12
  1006.0 0.3 fusion.45
  1006.3 5.1 fusion.41
  1011.4 1.5 fusion.3
  1013.0 0.3 convolution_add_fusion
  1013.2 0.4 convolution_add_fusion.3
  1013.7 0.2 add.102
  1013.9 0.4 convolution_reduce_fusion
  1014.3 0.1 multiply_add_fusion
  1014.4 20.4 %psum.69 = f32[8,576]{1,0:T(8,128)S(1)} all-reduce(f32[8,576]{1,0:T(8,128)S(1)} %multiply_add_fusion), channel_id=1, replica_groups=mesh['row'=8,'col'=8,'track'=4] {'row'}, use_global_device_ids=true, to_apply=%region_16.17 | all-reduce | flops 4608 | bytes 36864 | tf_op jit(solution)/shard_map/psum | solution.py:117
  1034.7 110.4 %psum.70 = f32[8,576]{1,0:T(8,128)S(1)} all-reduce(f32[8,576]{1,0:T(8,128)S(1)} %psum.69), channel_id=1, replica_groups=mesh['row'=8,'col'=8,'track'=4] {'col','track'}, use_global_device_ids=true, to_apply=%region_17.18 | all-reduce | flops 4608 | bytes 36864 | tf_op jit(solution)/shard_map/psum | solution.py:117
  1145.1 0.6 multiply_reduce_fusion
  1145.7 43.2 %psum.71 = f32[]{:T(128)} all-reduce(f32[]{:T(128)} %multiply_reduce_fusion), channel_id=1, replica_groups=mesh['row'=8,'col'=8,'track'=4] {'row'}, use_global_device_ids=true, to_apply=%region_19.20 | all-reduce | flops 1 | bytes 8 | tf_op jit(solution)/shard_map/psum | solution.py:122
  1190.3 0.6 subtract_divide_fusion
  (20 shorter events, 0.1 us)
Async XLA Ops:
  9.8 41.2 %all-to-all-start.1 = ((s32[64,1,3]{2,1,0:T(1,128)}), s32[64,1,3]{2,1,0:T(1,128)S(1)}, u32[]{:S(2)}, u32[]{:S(2)}) async-start(s32[64,1,3]{2,1,0:T(1,128)} %bitcast.21), calls=%async_computation.1 | async-start | bytes 65536 | tf_op jit(solution)/shard_map/all_to_all | solution.py:64
  51.0 10.8 copy-start.3
  51.1 359.4 %all-to-all-start = ((f32[64,3,2,16,576]{4,3,2,1,0:T(8,128)}), f32[64,3,2,16,576]{4,3,2,1,0:T(8,128)}, u32[]{:S(2)}, u32[]{:S(2)}) async-start(f32[64,3,2,16,576]{4,3,2,1,0:T(8,128)} %bitcast.149), calls=%async_computation | async-start | bytes 31457280 | tf_op jit(solution)/shard_map/all_to_all | solution.py:57
  61.8 725.8 %reduce-scatter.2.cloned.1.call-start = ((), (), s32[]{:S(2)}) async-start(), calls=%async_computation.3 | async-start | bytes 1843200 | tf_op jit(solution)/shard_map/reduce_scatter | solution.py:87
  418.1 337.9 %copy-start.1 = (f32[1,576]{1,0:T(1,128)S(1)}, f32[1,576]{1,0:T(1,128)}, u32[]{:S(2)}) copy-start(f32[1,576]{1,0:T(1,128)} %param.8) | copy-start | bytes 6916
  418.1 337.8 %copy-start.2 = (f32[1,576]{1,0:T(1,128)S(1)}, f32[1,576]{1,0:T(1,128)}, u32[]{:S(2)}) copy-start(f32[1,576]{1,0:T(1,128)} %param.9) | copy-start | bytes 6916
  783.9 227.5 %slice-start = ((s8[5242880]{0:T(1024)(128)(4,1)}), s8[1048576]{0:T(1024)(128)(4,1)S(1)}, s32[]{:S(2)}) async-start(s8[5242880]{0:T(1024)(128)(4,1)} %bitcast.147), calls=%async_computation.4 | async-start | bytes 2097152
  997.4 14.0 %slice-start.1 = ((s8[5242880]{0:T(1024)(128)(4,1)}), s8[4194304]{0:T(1024)(128)(4,1)S(1)}, s32[]{:S(2)}) async-start(s8[5242880]{0:T(1024)(128)(4,1)} %bitcast.147), calls=%async_computation.5 | async-start | bytes 8388608
  997.4 15.8 %copy-start = (f32[144,576]{1,0:T(8,128)S(1)}, f32[144,576]{1,0:T(8,128)}, u32[]{:S(2)}) copy-start(f32[144,576]{1,0:T(8,128)} %reduce-scatter.2.cloned.1.call-done) | copy-start | bytes 995332
Sparse Core Ops, SparseCore 0:
  665.8 38.9 reduce-scatter.1
